TPU v7x, 32 devices: a whole 2x2x4 slice. The times are simulated.
32 devices in a mesh: groups: 2 (over x), mesh: 16 (over z, y, core).
Axes of the slice: x: 2, y: 2, z: 4, core: 2. Of those that a mesh axis runs over, the one named last changes fastest.
Arguments:
- grid_in: bfloat16 [16384, 474], P(('groups', 'mesh')), parts along dimension 0, may hold values from -6 to 6
- owner: int32 [8192, 1], P('mesh'), may hold values from 0 to 15; in each aligned block of 512 rows (0 to 511, 512 to 1023, ...) at most 64 rows name the same one
- node_slot: int32 [8192], P('mesh'), may hold values from 0 to 255
- mesh_embed: bfloat16 [8192, 512], P(('groups', 'mesh')), parts along dimension 0, may hold values from -6 to 6
- edge_latent: bfloat16 [65536, 512], P(('groups', 'mesh')), parts along dimension 0, may hold values from -6 to 6
- senders: int32 [32768], P('mesh'), may hold values from 0 to 767
- receivers: int32 [32768], P('mesh'), may hold values from 0 to 255
- send_list: int32 [256, 32], P('mesh'), may hold values from 0 to 255
- w_grid_first: bfloat16 [474, 512], replicated, may hold values from -0.25 to 0.25
- w_grid_second: bfloat16 [512, 512], replicated, may hold values from -0.25 to 0.25
- w_enc_first: bfloat16 [1024, 512], replicated, may hold values from -0.1875 to 0.1875
- w_enc_second: bfloat16 [512, 512], replicated, may hold values from -0.25 to 0.25
- w_send: bfloat16 [512, 512], replicated, may hold values from -0.15625 to 0.15625
- w_recv: bfloat16 [512, 512], replicated, may hold values from -0.15625 to 0.15625
- w_edge: bfloat16 [512, 512], replicated, may hold values from -0.15625 to 0.15625
- w_message: bfloat16 [512, 512], replicated, may hold values from -0.25 to 0.25
- w_proc_first: bfloat16 [1024, 512], replicated, may hold values from -0.1875 to 0.1875
- w_proc_second: bfloat16 [512, 512], replicated, may hold values from -0.25 to 0.25
Outputs:
- mesh_out: bfloat16 [8192, 512], P(('groups', 'mesh')), parts along dimension 0
There are 2 independent parts, one for each index of `groups`. A program takes and returns all parts, laid end to end along the dimension named above; an argument that names none is the same for every part. Nothing has to cross between parts.
Inputs may be any that keep to these rules, and one draw needn't show every extreme that they name: Among the grid points of one device at most 64 have the same owner, and some device has exactly 64 with one owner. Grid point g feeds node row node_slot[g] of device owner[g]. `senders`: A sender below 256 is a node row of the edge's own device; a sender 256 + p * 32 + j is row send_list[p * 16 + q, j] of device p, where q is the edge's device. `receivers`: edge k lies on device k // 2048; its receiver is a node row of that device. `send_list`: row p * 16 + q lists the 32 node rows of device p sent to device q.
All inputs are finite; a program needn't handle non-finite values.
Results may differ from a plain program's by a relative error of at most 0.0095.
Values may be sent and summed in bfloat16 or wider, within the bound.
A program may use at most 64 MiB of HBM per device.

v0:
```python
import jax
import jax.numpy as jnp
from jax import lax
from jax.sharding import PartitionSpec as P


def layer_norm(values):
    center = values - jnp.mean(values, -1, keepdims=True)
    spread = jnp.mean(center * center, -1, keepdims=True)
    return center * lax.rsqrt(spread + 1e-05)


def embed_grid(grid_rows, w_first, w_second):
    hidden = jax.nn.silu(jnp.dot(grid_rows, w_first, preferred_element_type=jnp.float32)).astype(
        jnp.bfloat16
    )
    return layer_norm(jnp.dot(hidden, w_second, preferred_element_type=jnp.float32)).astype(
        jnp.bfloat16
    )


def update_nodes(state, gathered, w_first, w_second):
    joined = jnp.concatenate([state.astype(jnp.float32), gathered], -1)
    normed = layer_norm(joined).astype(jnp.bfloat16)
    hidden = jax.nn.silu(jnp.dot(normed, w_first, preferred_element_type=jnp.float32)).astype(
        jnp.bfloat16
    )
    return (
        state.astype(jnp.float32) + jnp.dot(hidden, w_second, preferred_element_type=jnp.float32)
    ).astype(jnp.bfloat16)


def per_device(
    grid_in,
    owner,
    node_slot,
    mesh_embed,
    edge_latent,
    senders,
    receivers,
    send_list,
    w_grid_first,
    w_grid_second,
    w_enc_first,
    w_enc_second,
    w_send,
    w_recv,
    w_edge,
    w_message,
    w_proc_first,
    w_proc_second,
):
    peer_count = lax.axis_size("mesh")
    grid_count = grid_in.shape[0]
    slot_count = 2 * grid_count // peer_count
    node_count = mesh_embed.shape[0]
    latent_width = w_grid_second.shape[1]
    target = owner[:, 0]
    peer_flags = (target[:, None] == jnp.arange(peer_count, dtype=jnp.int32)[None, :]).astype(
        jnp.int32
    )
    slot_rank = jnp.sum((jnp.cumsum(peer_flags, 0) - peer_flags) * peer_flags, 1)
    position = target * slot_count + slot_rank
    node_ids = (
        jnp.full((peer_count * slot_count,), node_count, jnp.int32).at[position].set(node_slot)
    )
    node_ids = node_ids.reshape(peer_count, slot_count)
    grid_latent = embed_grid(grid_in, w_grid_first, w_grid_second)
    outgoing = (
        jnp.zeros((peer_count * slot_count, latent_width), jnp.bfloat16)
        .at[position]
        .set(grid_latent)
    )
    arrived, arrived_ids = (
        lax.all_to_all(
            outgoing.reshape(peer_count, slot_count, latent_width),
            "mesh",
            split_axis=0,
            concat_axis=0,
            tiled=True,
        ),
        lax.all_to_all(node_ids, "mesh", split_axis=0, concat_axis=0, tiled=True),
    )
    node_rows = jnp.arange(node_count, dtype=jnp.int32)
    slot_table = (node_rows[:, None] == arrived_ids.reshape(1, peer_count * slot_count)).astype(
        jnp.bfloat16
    )
    g2m_sum = jnp.dot(
        slot_table,
        arrived.reshape(peer_count * slot_count, latent_width),
        preferred_element_type=jnp.float32,
    )
    mesh_latent = update_nodes(mesh_embed, g2m_sum, w_enc_first, w_enc_second)
    halo_out = mesh_latent[send_list]
    incoming = lax.all_to_all(halo_out, "mesh", split_axis=0, concat_axis=0, tiled=True)
    halo_rows = incoming.reshape(incoming.shape[0] * incoming.shape[1], latent_width)
    node_table = jnp.concatenate([mesh_latent, halo_rows], 0)
    edge_pre = jnp.dot(node_table[senders], w_send, preferred_element_type=jnp.float32)
    edge_pre = edge_pre + jnp.dot(
        mesh_latent[receivers], w_recv, preferred_element_type=jnp.float32
    )
    edge_pre = edge_pre + jnp.dot(edge_latent, w_edge, preferred_element_type=jnp.float32)
    edge_hidden = jax.nn.silu(edge_pre).astype(jnp.bfloat16)
    message = jnp.dot(edge_hidden, w_message, preferred_element_type=jnp.float32)
    edge_table = (node_rows[:, None] == receivers[None, :]).astype(jnp.float32)
    node_sum = jnp.dot(
        edge_table, message, precision=lax.Precision.HIGHEST, preferred_element_type=jnp.float32
    )
    return update_nodes(mesh_latent, node_sum, w_proc_first, w_proc_second)


def solution(mesh):
    in_specs = (
        P(("groups", "mesh"), None),
        P("mesh", None),
        P("mesh"),
        P(("groups", "mesh"), None),
        P(("groups", "mesh"), None),
        P("mesh"),
        P("mesh"),
        P("mesh", None),
        P(),
        P(),
        P(),
        P(),
        P(),
        P(),
        P(),
        P(),
        P(),
        P(),
    )
    out_specs = P(("groups", "mesh"), None)
    return jax.shard_map(
        per_device, mesh=mesh, in_specs=in_specs, out_specs=out_specs, check_vma=False
    )
```

profile of v0, /device:TPU:0, one launch (start us, length us, event | category | flops | bytes accessed | tf_op | source)
XLA Modules:
  0.0 112.8 jit_solution(16554895026261246798)
XLA Ops:
  0.0 0.8 fusion.25
  0.8 1.1 %reduce-window.6 = s32[16,4,128]{2,0,1:T(8,128)S(1)} reduce-window(s32[16,4,128]{2,0,1:T(8,128)S(1)} %fusion.25, s32[]{:T(128)} %constant.15.clone.1), window={size=1x1x128 pad=0_0x0_0x127_0}, to_apply=%region_0.0 | reduce-window | flops 1040384 | bytes 65540 | tf_op jit(solution)/shard_map/reduce-window
  2.2 0.8 fusion.24
  3.7 2.6 %scatter_custom_fusion = s32[1024]{0:T(1024)S(1)} fusion(s32[512]{0:T(512)S(1)} %bitcast.49, s32[512]{0:T(512)} %param.20, s32[]{:T(128)} %constant.13.clone.1), kind=kCustom, calls=%fused_computation.59 | custom fusion | bytes 4608 | tf_op jit(solution)/shard_map/scatter | solution.py:65
  7.0 7.4 %all-to-all-start = ((s32[16,1,64]{2,1,0:T(1,128)}), s32[16,1,64]{2,1,0:T(1,128)S(1)}, u32[]{:S(2)}, u32[]{:S(2)}) async-start(s32[16,1,64]{2,1,0:T(1,128)} %all_to_all.12), calls=%async_computation | async-start | bytes 16384 | tf_op jit(solution)/shard_map/all_to_all | solution.py:82
  14.4 2.4 %fusion.38 = (f32[512]{0:T(512)S(1)}, f32[512,512]{0,1:T(8,128)S(1)}) fusion(bf16[512,512]{1,0:T(8,128)(2,1)} %param.27, bf16[512,474]{0,1:T(8,128)(2,1)} %param.18, bf16[474,512]{1,0:T(8,128)(2,1)} %param.26), kind=kOutput, calls=%fused_computation.72 | convolution fusion | flops 518520320 | bytes 2545664 | tf_op jit(solution)/shard_map/dot_general | solution.py:17
  17.0 0.9 multiply_convert_fusion.3
  17.9 1.3 %copy.20 = bf16[512,512]{1,0:T(8,128)(2,1)S(1)} copy(bf16[512,512]{0,1:T(8,128)(2,1)} %multiply_convert_fusion.3) | data formatting | bytes 1048576 | tf_op jit(solution)/shard_map/convert_element_type | solution.py:17
  19.2 3.5 %scatter_custom_fusion.1 = bf16[1024,512]{1,0:T(8,128)(2,1)} fusion(s32[512]{0:T(512)S(1)} %bitcast.50, bf16[512,512]{1,0:T(8,128)(2,1)S(1)} %copy.20, bf16[]{:T(256)} %constant.18.clone.1), kind=kCustom, calls=%fused_computation.34 | custom fusion | bytes 1048578 | tf_op jit(solution)/shard_map/scatter | solution.py:72
  22.7 6.1 %all-to-all-start.1 = ((bf16[16,64,512]{2,1,0:T(8,128)(2,1)}), bf16[16,64,512]{2,1,0:T(8,128)(2,1)}, u32[]{:S(2)}, u32[]{:S(2)}) async-start(bf16[16,64,512]{2,1,0:T(8,128)(2,1)} %bitcast.5), calls=%async_computation.1 | async-start | bytes 2097152 | tf_op jit(solution)/shard_map/all_to_all | solution.py:75
  30.3 21.4 %all-to-all-done.1 = bf16[16,64,512]{2,1,0:T(8,128)(2,1)} async-done(((bf16[16,64,512]{2,1,0:T(8,128)(2,1)}), bf16[16,64,512]{2,1,0:T(8,128)(2,1)}, u32[]{:S(2)}, u32[]{:S(2)}) %all-to-all-start.1) | async-done | bytes 1048608 | tf_op jit(solution)/shard_map/all_to_all | solution.py:75
  51.8 1.7 %fusion.39 = (f32[256]{0:T(256)S(1)}, f32[256,512]{1,0:T(8,128)S(1)}) fusion(bf16[1024,512]{1,0:T(8,128)(2,1)} %bitcast.6, s32[1024]{0:T(1024)S(1)} %eq.62), kind=kOutput, calls=%fused_computation.73 | convolution fusion | flops 268828416 | bytes 1577984 | tf_op jit(solution)/shard_map/dot_general | solution.py:88
  53.8 3.0 %fusion.40 = (f32[256,512]{1,0:T(8,128)}, bf16[256,512]{1,0:T(8,128)(2,1)S(1)}) fusion(f32[256,512]{1,0:T(8,128)S(1)} %convert_element_type.44, bf16[512,512]{1,0:T(8,128)(2,1)} %param.29, bf16[1024,512]{1,0:T(8,128)(2,1)} %param.28, f32[256,512]{1,0:T(8,128)S(1)} %get-tuple-element.8, f32[256]{0:T(256)S(1)} %add_rsqrt_fusion.2, f32[256]{0:T(256)S(1)} %add_multiply_fusion.1), kind=kOutput, calls=%fused_computation.74 | convolution fusion | flops 404750336 | bytes 3409920 | tf_op jit(solution)/shard_map/dot_general | solution.py:29
  56.8 2.6 %gather_fusion = bf16[512,512]{1,0:T(8,128)(2,1)} fusion(bf16[256,512]{1,0:T(8,128)(2,1)S(1)} %get-tuple-element.10, s32[1024]{0:T(1024)S(1)} %pad_clamp_fusion), kind=kCustom, calls=%fused_computation | custom fusion | bytes 1050624 | tf_op jit(solution)/shard_map/gather | solution.py:94
  59.4 6.9 %all-to-all-start.2 = ((bf16[16,32,512]{2,1,0:T(8,128)(2,1)}), bf16[16,32,512]{2,1,0:T(8,128)(2,1)S(1)}, u32[]{:S(2)}, u32[]{:S(2)}) async-start(bf16[16,32,512]{2,1,0:T(8,128)(2,1)} %bitcast.7), calls=%async_computation.2 | async-start | bytes 1048576 | tf_op jit(solution)/shard_map/all_to_all | solution.py:95
  66.3 9.2 %gather_fusion.2 = bf16[2048,512]{1,0:T(8,128)(2,1)} fusion(bf16[256,512]{1,0:T(8,128)(2,1)S(1)} %get-tuple-element.10, s32[2048]{0:T(1024)S(1)} %fusion.27), kind=kCustom, calls=%fused_computation.2 | custom fusion | bytes 4202496 | tf_op jit(solution)/shard_map/gather | solution.py:100
  75.6 4.8 %fusion.45 = f32[2048,512]{1,0:T(8,128)} fusion(bf16[2048,512]{1,0:T(8,128)(2,1)} %gather_fusion.2, bf16[512,512]{1,0:T(8,128)(2,1)S(1)} %copy-done.3), kind=kOutput, calls=%fused_computation.78 | convolution fusion | flops 1073741824 | bytes 6815744 | tf_op jit(solution)/shard_map/dot_general | solution.py:99
  80.7 0.8 copy-done.1
  81.5 1.1 pad_maximum_fusion
  82.6 9.2 %gather_fusion.1 = bf16[2048,512]{1,0:T(8,128)(2,1)} fusion(bf16[768,512]{1,0:T(8,128)(2,1)S(1)} %pad_maximum_fusion, s32[2048]{0:T(1024)S(1)} %fusion.26), kind=kCustom, calls=%fused_computation.1 | custom fusion | bytes 4202496 | tf_op jit(solution)/shard_map/gather | solution.py:98
  91.8 5.0 %fusion.44 = f32[2048,512]{1,0:T(8,128)} fusion(bf16[2048,512]{1,0:T(8,128)(2,1)} %gather_fusion.1, bf16[512,512]{1,0:T(8,128)(2,1)} %param.30), kind=kOutput, calls=%fused_computation.77 | convolution fusion | flops 1073741824 | bytes 6815744 | tf_op jit(solution)/shard_map/dot_general | solution.py:98
  96.8 8.3 %fusion.1 = f32[2048,512]{1,0:T(8,128)} fusion(bf16[512,512]{1,0:T(8,128)(2,1)S(1)} %copy-done.8, f32[2048,512]{1,0:T(8,128)} %fusion.44, f32[2048,512]{1,0:T(8,128)} %fusion.45, bf16[2048,512]{1,0:T(8,128)(2,1)S(1)} %copy-done, bf16[512,512]{1,0:T(8,128)(2,1)S(1)} %copy-done.9), kind=kOutput, calls=%fused_computation.8 | convolution fusion | flops 2154823680 | bytes 15728640 | tf_op jit(solution)/shard_map/dot_general | solution.py:104
  105.0 4.7 %fusion.41 = (f32[256]{0:T(256)S(1)}, f32[256,512]{1,0:T(8,128)S(1)}) fusion(f32[2048,512]{1,0:T(8,128)} %fusion.1, s32[2048]{0:T(1024)S(1)} %copy-done.5), kind=kOutput, calls=%fused_computation.75 | convolution fusion | flops 3221880576 | bytes 4727808 | tf_op jit(solution)/shard_map/dot_general | solution.py:106
  110.0 2.8 %fusion.3 = bf16[256,512]{1,0:T(8,128)(2,1)} fusion(f32[256,512]{1,0:T(8,128)S(1)} %copy-done.4, bf16[512,512]{1,0:T(8,128)(2,1)} %param.35, bf16[1024,512]{1,0:T(8,128)(2,1)} %param.34, f32[256,512]{1,0:T(8,128)S(1)} %get-tuple-element.12, f32[256]{0:T(256)S(1)} %add_rsqrt_fusion.1, f32[256]{0:T(256)S(1)} %add_multiply_fusion), kind=kOutput, calls=%fused_computation.12 | convolution fusion | flops 404619264 | bytes 2885632 | tf_op jit(solution)/shard_map/dot_general | solution.py:29
  (46 shorter events, 4.3 us)
Async XLA Ops:
  0.0 96.8 %copy-start = (bf16[2048,512]{1,0:T(8,128)(2,1)S(1)}, bf16[2048,512]{1,0:T(8,128)(2,1)}, u32[]{:S(2)}) copy-start(bf16[2048,512]{1,0:T(8,128)(2,1)} %param.22) | copy-start | bytes 6291460
  7.0 15.7 %all-to-all-start = ((s32[16,1,64]{2,1,0:T(1,128)}), s32[16,1,64]{2,1,0:T(1,128)S(1)}, u32[]{:S(2)}, u32[]{:S(2)}) async-start(s32[16,1,64]{2,1,0:T(1,128)} %all_to_all.12), calls=%async_computation | async-start | bytes 16384 | tf_op jit(solution)/shard_map/all_to_all | solution.py:82
  17.9 10.9 %copy-start.6 = (s32[16,32]{1,0:T(8,128)S(1)}, s32[16,32]{1,0:T(8,128)}, u32[]{:S(2)}) copy-start(s32[16,32]{1,0:T(8,128)} %param.25) | copy-start | bytes 6148
  17.9 11.0 %copy-start.2 = (bf16[256,512]{1,0:T(8,128)(2,1)S(1)}, bf16[256,512]{1,0:T(8,128)(2,1)}, u32[]{:S(2)}) copy-start(bf16[256,512]{1,0:T(8,128)(2,1)} %param.21) | copy-start | bytes 786436
  22.7 29.1 %all-to-all-start.1 = ((bf16[16,64,512]{2,1,0:T(8,128)(2,1)}), bf16[16,64,512]{2,1,0:T(8,128)(2,1)}, u32[]{:S(2)}, u32[]{:S(2)}) async-start(bf16[16,64,512]{2,1,0:T(8,128)(2,1)} %bitcast.5), calls=%async_computation.1 | async-start | bytes 2097152 | tf_op jit(solution)/shard_map/all_to_all | solution.py:75
  56.8 9.5 %copy-start.7 = (s32[2048]{0:T(1024)S(1)}, s32[2048]{0:T(1024)}, u32[]{:S(2)}) copy-start(s32[2048]{0:T(1024)} %param.23) | copy-start | bytes 24580
  56.8 9.5 %copy-start.5 = (s32[2048]{0:T(1024)S(1)}, s32[2048]{0:T(1024)}, u32[]{:S(2)}) copy-start(s32[2048]{0:T(1024)} %param.24) | copy-start | bytes 24580
  59.4 21.3 %all-to-all-start.2 = ((bf16[16,32,512]{2,1,0:T(8,128)(2,1)}), bf16[16,32,512]{2,1,0:T(8,128)(2,1)S(1)}, u32[]{:S(2)}, u32[]{:S(2)}) async-start(bf16[16,32,512]{2,1,0:T(8,128)(2,1)} %bitcast.7), calls=%async_computation.2 | async-start | bytes 1048576 | tf_op jit(solution)/shard_map/all_to_all | solution.py:95
  66.3 9.3 %copy-start.3 = (bf16[512,512]{1,0:T(8,128)(2,1)S(1)}, bf16[512,512]{1,0:T(8,128)(2,1)}, u32[]{:S(2)}) copy-start(bf16[512,512]{1,0:T(8,128)(2,1)} %param.31) | copy-start | bytes 1572868
  80.7 0.8 copy-start.1
  91.8 5.0 %copy-start.8 = (bf16[512,512]{1,0:T(8,128)(2,1)S(1)}, bf16[512,512]{1,0:T(8,128)(2,1)}, u32[]{:S(2)}) copy-start(bf16[512,512]{1,0:T(8,128)(2,1)} %param.33) | copy-start | bytes 1572868
  91.8 5.0 %copy-start.9 = (bf16[512,512]{1,0:T(8,128)(2,1)S(1)}, bf16[512,512]{1,0:T(8,128)(2,1)}, u32[]{:S(2)}) copy-start(bf16[512,512]{1,0:T(8,128)(2,1)} %param.32) | copy-start | bytes 1572868
  105.0 4.7 %copy-start.4 = (f32[256,512]{1,0:T(8,128)S(1)}, f32[256,512]{1,0:T(8,128)}, u32[]{:S(2)}) copy-start(f32[256,512]{1,0:T(8,128)} %get-tuple-element.9) | copy-start | bytes 1572868
where the time goes:
time: 113 us
  matrix products  32.6 us (29%)
  local copies, waits for them, and re-layouts  30.8 us (27%)
  waiting for transfers between devices  21.8 us (19%)
  starting transfers between devices  20.3 us (18%)
  other arithmetic  7.18 us (6%)
    all_to_all x1, waiting for transfers between devices, per_device(): lax.all_to_all(outgoing.reshape(peer_count, slot_count, latent_width), 'm...  21.4 us
    gather x1, local copies, waits for them, and re-layouts, per_device(): mesh_latent[receivers]  9.18 us
    gather x1, local copies, waits for them, and re-layouts, per_device(): node_table[senders]  9.16 us
    dot_general x1, matrix products, per_device(): jnp.dot(edge_hidden, w_message, preferred_element_type=jnp.float32)  8.26 us
    all_to_all x1, starting transfers between devices, per_device(): lax.all_to_all(node_ids, 'mesh', split_axis=0, concat_axis=0, tiled=True)  7.39 us
    all_to_all x1, starting transfers between devices, per_device(): lax.all_to_all(halo_out, 'mesh', split_axis=0, concat_axis=0, tiled=True)  6.88 us
    all_to_all x1, starting transfers between devices, per_device(): lax.all_to_all(outgoing.reshape(peer_count, slot_count, latent_width), 'm...  6.06 us
    dot_general x2, matrix products, update_nodes(): jnp.dot(hidden, w_second, preferred_element_type=jnp.float32)  5.79 us
  transfers between devices with their start and end apart: 3, of which 2 were waited for; matrix products, arithmetic and copies ran while one was open for 21% of the time, Pallas kernels for 0%

commit v1 on v0

v1 whole, which is shorter than its diff:
```python
import functools

import jax
import jax.numpy as jnp
from jax import lax
from jax.experimental import pallas as pl
from jax.experimental.pallas import tpu as pltpu
from jax.sharding import PartitionSpec as P

F32 = jnp.float32
BF16 = jnp.bfloat16
MESH = pl.DeviceIdType.MESH
GROUP = 256
CHUNK = 256
LANES = 128


def dot(left, right):
    return jnp.dot(left, right, preferred_element_type=F32)


def silu(x):
    half = 0.5 * x
    return half * jnp.tanh(half) + half


def normalize(values):
    center = values - jnp.mean(values, -1, keepdims=True)
    spread = jnp.mean(center * center, -1, keepdims=True)
    return center * lax.rsqrt(spread + 1e-05)


def hot(flags):
    return jnp.where(flags, 1.0, 0.0).astype(BF16)


def update(state, gathered, w_first, w_second):
    width = state.shape[1]
    rows = state.astype(F32)
    mean = (
        jnp.sum(rows, -1, keepdims=True) + jnp.sum(gathered, -1, keepdims=True)
    ) / (2 * width)
    low, high = rows - mean, gathered - mean
    spread = (
        jnp.sum(low * low, -1, keepdims=True) + jnp.sum(high * high, -1, keepdims=True)
    ) / (2 * width)
    scale = lax.rsqrt(spread + 1e-05)
    hidden = dot((low * scale).astype(BF16), w_first[:width, :])
    hidden = hidden + dot((high * scale).astype(BF16), w_first[width:, :])
    return (rows + dot(silu(hidden).astype(BF16), w_second[...])).astype(BF16)


def kernel(n, cap, hcap, *refs):
    hbm = refs[:18]
    out_ref = refs[18]
    (
        grid_in,
        owner,
        node_slot,
        embed,
        edges,
        senders,
        receivers,
        send_list,
        w_grid_first,
        w_grid_second,
        w_enc_first,
        w_enc_second,
        w_send,
        w_recv,
        w_edge,
        w_message,
        w_proc_first,
        w_proc_second,
    ) = vmem = refs[19:37]
    (
        latent,
        outgoing,
        arrived,
        ids_out,
        ids_in,
        pre,
        local_table,
        near_hot,
        halo_hot,
        node_hot,
        list_hot,
        halo_out,
        halo_in,
        load_sem,
        row_send,
        row_recv,
        id_send,
        id_recv,
        halo_send,
        halo_recv,
    ) = refs[37:]
    grid_count = grid_in.shape[0]
    nodes, width = embed.shape
    edge_count = edges.shape[0]
    me = lax.axis_index("mesh")

    def offset(t):
        return n // 2 - (t + 1) // 2 if t % 2 else n // 2 + t // 2

    def peer(t):
        return lax.rem(me + offset(t), n)

    loads = [
        pltpu.make_async_copy(source, target, load_sem.at[i])
        for i, (source, target) in enumerate(zip(hbm, vmem))
    ]
    for i in (0, 8, 1, 2, 9, 14, 4, 3, 10, 11, 7, 12, 13, 5, 6, 15, 16, 17):
        loads[i].start()
    barrier = pltpu.get_barrier_semaphore()
    for t in range(n - 1):
        pl.semaphore_signal(barrier, inc=1, device_id={"mesh": peer(t)}, device_id_type=MESH)

    loads[1].wait()
    loads[2].wait()
    step = lax.broadcasted_iota(jnp.int32, (n, 1), 0)
    turn = n // 2 + jnp.where(step % 2 == 1, -((step + 1) // 2), step // 2)
    target = lax.rem(me + turn, n)
    flags = jnp.where(target == owner[...], 1.0, 0.0)
    earlier = hot(
        lax.broadcasted_iota(jnp.int32, (grid_count, grid_count), 0)
        < lax.broadcasted_iota(jnp.int32, (grid_count, grid_count), 1)
    )
    rank = dot(flags.astype(BF16), earlier) + (step * cap).astype(F32)
    place = jnp.sum(flags * rank, 0, keepdims=True).astype(jnp.int32)
    slots = (flags * (node_slot[...] + 1).astype(F32)).astype(BF16)
    lane_hot = hot(
        lax.broadcasted_iota(jnp.int32, (GROUP, grid_count), 0) == place % GROUP
    )
    ids = lax.dot_general(slots, lane_hot, (((1,), (1,)), ((), ())), preferred_element_type=F32)
    for t in range(n):
        ids_out[t] = ids[t : t + 1, :]
    ids_in[n - 1] = ids[n - 1 : n, :]

    loads[0].wait()
    loads[8].wait()
    loads[9].wait()
    hidden = silu(dot(grid_in[...], w_grid_first[...])).astype(BF16)
    latent[...] = normalize(dot(hidden, w_grid_second[...])).astype(BF16)

    pl.semaphore_wait(barrier, n - 1)
    per_group = GROUP // cap
    copies = []
    for group in range(n // per_group):
        pack = hot(
            lax.broadcasted_iota(jnp.int32, (GROUP, grid_count), 0) + group * GROUP == place
        )
        block = dot(pack, latent[...]).astype(BF16)
        first = group * per_group
        outgoing[first : first + per_group] = block.reshape(per_group, cap, width)
        for t in range(first, min(first + per_group, n - 1)):
            id_copy = pltpu.make_async_remote_copy(
                src_ref=ids_out.at[t],
                dst_ref=ids_in.at[t],
                send_sem=id_send.at[t],
                recv_sem=id_recv.at[t],
                device_id={"mesh": peer(t)},
                device_id_type=MESH,
            )
            row_copy = pltpu.make_async_remote_copy(
                src_ref=outgoing.at[t],
                dst_ref=arrived.at[t],
                send_sem=row_send.at[t],
                recv_sem=row_recv.at[t],
                device_id={"mesh": peer(t)},
                device_id_type=MESH,
            )
            id_copy.start()
            row_copy.start()
            copies.append((id_copy, row_copy))
    arrived[n - 1] = outgoing[n - 1]

    loads[14].wait()
    loads[4].wait()
    for chunk in range(edge_count // CHUNK):
        rows = pl.ds(chunk * CHUNK, CHUNK)
        pre[rows, :] = dot(edges[rows, :], w_edge[...])
    loads[5].wait()
    loads[6].wait()
    loads[7].wait()
    sender_columns = jnp.transpose(senders[...])
    receiver_columns = jnp.transpose(receivers[...])
    list_columns = jnp.transpose(send_list[...])
    near_iota = lax.broadcasted_iota(jnp.int32, (LANES, nodes), 1)
    halo_iota = lax.broadcasted_iota(jnp.int32, (LANES, n * hcap), 1) + nodes
    node_iota = lax.broadcasted_iota(jnp.int32, (nodes, LANES), 0)
    for part in range(edge_count // LANES):
        rows = pl.ds(part * LANES, LANES)
        sender = sender_columns[:, part : part + 1]
        receiver = receiver_columns[:, part : part + 1]
        near_hot[rows, :nodes] = hot(sender == near_iota)
        near_hot[rows, nodes:] = hot(receiver == near_iota)
        halo_hot[rows, :] = hot(sender == halo_iota)
        node_hot[:, part * LANES : (part + 1) * LANES] = hot(
            receivers[part : part + 1, :] == node_iota
        )
    list_iota = lax.broadcasted_iota(jnp.int32, (hcap, nodes), 1)
    for p in range(n):
        list_hot[p * hcap : (p + 1) * hcap, :] = hot(list_columns[:, p : p + 1] == list_iota)

    gathered = jnp.zeros((nodes, width), F32)
    slot_iota = lax.broadcasted_iota(jnp.int32, (nodes, GROUP), 0).astype(F32) + 1.0
    for group in range(n // per_group):
        first = group * per_group
        named = jnp.zeros((1, GROUP), F32)
        for t in range(first, first + per_group):
            if t < n - 1:
                copies[t][0].wait_recv()
                copies[t][1].wait_recv()
            named = named + ids_in[t]
        gathered = gathered + dot(
            hot(slot_iota == named),
            arrived[first : first + per_group].reshape(GROUP, width),
        )

    for i in (3, 10, 11, 12, 13):
        loads[i].wait()
    state = update(embed[...], gathered, w_enc_first, w_enc_second)
    sent = dot(state, w_send[...]).astype(BF16)
    halo_out[...] = dot(list_hot[...], sent).astype(BF16).reshape(n, hcap, width)
    halo_copies = []
    for t in range(n - 1):
        copy = pltpu.make_async_remote_copy(
            src_ref=halo_out.at[peer(t)],
            dst_ref=halo_in.at[me],
            send_sem=halo_send.at[t],
            recv_sem=halo_recv.at[t],
            device_id={"mesh": peer(t)},
            device_id_type=MESH,
        )
        copy.start()
        halo_copies.append(copy)
    halo_in[me] = halo_out[me]
    local_table[:nodes, :] = sent
    local_table[nodes:, :] = dot(state, w_recv[...]).astype(BF16)
    for chunk in range(edge_count // CHUNK):
        rows = pl.ds(chunk * CHUNK, CHUNK)
        pre[rows, :] += dot(near_hot[rows, :], local_table[...])

    for copy in halo_copies:
        copy.wait_recv()
    halo = halo_in[...].reshape(n * hcap, width)
    summed = jnp.zeros((nodes, width), F32)
    for chunk in range(edge_count // CHUNK):
        rows = pl.ds(chunk * CHUNK, CHUNK)
        edge_pre = pre[rows, :] + dot(halo_hot[rows, :], halo)
        summed = summed + dot(
            node_hot[:, chunk * CHUNK : (chunk + 1) * CHUNK], silu(edge_pre).astype(BF16)
        )
    for i in (15, 16, 17):
        loads[i].wait()
    node_sum = dot(summed.astype(BF16), w_message[...])
    out_ref[...] = update(state, node_sum, w_proc_first, w_proc_second)
    for id_copy, row_copy in copies:
        id_copy.wait_send()
        row_copy.wait_send()
    for copy in halo_copies:
        copy.wait_send()


def per_device(
    grid_in, owner, node_slot, mesh_embed, edge_latent, senders, receivers, send_list, *weights
):
    n = lax.axis_size("mesh")
    grid_count = grid_in.shape[0]
    nodes, width = mesh_embed.shape
    edge_count = edge_latent.shape[0]
    list_size = send_list.shape[1]
    cap = max(16, 2 * grid_count // n)
    hcap = max(16, list_size)
    if hcap != list_size:
        beyond = jnp.maximum(senders - nodes, 0)
        moved = nodes + beyond // list_size * hcap + beyond % list_size
        senders = jnp.where(senders < nodes, senders, moved)
        send_list = jnp.pad(send_list, ((0, 0), (0, hcap - list_size)))
    inputs = (
        grid_in,
        owner.reshape(1, grid_count),
        node_slot.reshape(1, grid_count),
        mesh_embed,
        edge_latent,
        senders.reshape(edge_count // LANES, LANES),
        receivers.reshape(edge_count // LANES, LANES),
        send_list,
    ) + weights
    dma = pltpu.SemaphoreType.DMA
    scratch = [pltpu.VMEM(x.shape, x.dtype) for x in inputs] + [
        pltpu.VMEM((grid_count, width), BF16),
        pltpu.VMEM((n, cap, width), BF16),
        pltpu.VMEM((n, cap, width), BF16),
        pltpu.VMEM((n, 1, GROUP), F32),
        pltpu.VMEM((n, 1, GROUP), F32),
        pltpu.VMEM((edge_count, width), F32),
        pltpu.VMEM((2 * nodes, width), BF16),
        pltpu.VMEM((edge_count, 2 * nodes), BF16),
        pltpu.VMEM((edge_count, n * hcap), BF16),
        pltpu.VMEM((nodes, edge_count), BF16),
        pltpu.VMEM((n * hcap, nodes), BF16),
        pltpu.VMEM((n, hcap, width), BF16),
        pltpu.VMEM((n, hcap, width), BF16),
        dma((len(inputs),)),
        dma((n,)),
        dma((n,)),
        dma((n,)),
        dma((n,)),
        dma((n,)),
        dma((n,)),
    ]
    return pl.pallas_call(
        functools.partial(kernel, n, cap, hcap),
        out_shape=jax.ShapeDtypeStruct((nodes, width), BF16),
        in_specs=[pl.BlockSpec(memory_space=pl.ANY)] * len(inputs),
        out_specs=pl.BlockSpec(memory_space=pltpu.VMEM),
        scratch_shapes=scratch,
        compiler_params=pltpu.CompilerParams(
            collective_id=0, has_side_effects=True, vmem_limit_bytes=56 << 20
        ),
    )(*inputs)


def solution(mesh):
    rows, split, full = P(("groups", "mesh"), None), P("mesh"), P()
    in_specs = (rows, split, split, rows, rows, split, split, split) + (full,) * 10
    return jax.shard_map(
        per_device, mesh=mesh, in_specs=in_specs, out_specs=rows, check_vma=False
    )
```

time: 113 us -> 53.1 us (0.47)
  Pallas kernels: 0 us -> 49.3 us
  matrix products: 32.6 us -> 0 us
  local copies, waits for them, and re-layouts: 30.8 us -> 3.7 us
  waiting for transfers between devices: 21.8 us -> 0 us
  starting transfers between devices: 20.3 us -> 0 us
  other arithmetic: 7.18 us -> 0 us
    pallas_call x0 -> x1, Pallas kernels: none -> 49.3 us  [per_device(): pl.pallas_call(functools.partial(kernel, n, cap, hcap), out_shape=jax.Sha...]
    dot_general x8 -> x0, matrix products: 32.6 us -> none  [the longest x1 8.26 us: per_device(): jnp.dot(edge_hidden, w_message, preferred_element_type=jnp.float32)]
    all_to_all x3 -> x0, waiting for transfers between devices: 21.8 us -> none  [the longest x1 21.4 us: per_device(): lax.all_to_all(outgoing.reshape(peer_count, slot_count, latent_width), 'm...]
    gather x3 -> x0, local copies, waits for them, and re-layouts: 21 us -> none  [the longest x1 9.18 us: per_device(): mesh_latent[receivers]]
    all_to_all x3 -> x0, starting transfers between devices: 20.3 us -> none  [the longest x1 7.39 us: per_device(): lax.all_to_all(node_ids, 'mesh', split_axis=0, concat_axis=0, tiled=True)]
    scatter x2 -> x0, local copies, waits for them, and re-layouts: 6.13 us -> none  [the longest x1 3.53 us: per_device(): outgoing = jnp.zeros((peer_count * slot_count, latent_width), jnp.bfloat1...]
    unnamed x20 -> x2, local copies, waits for them, and re-layouts: 0.83 us -> 3.7 us
    convert_element_type x3 -> x0, other arithmetic: 1.81 us -> none  [the longest x1 0.93 us: embed_grid(): layer_norm(jnp.dot(hidden, w_second, preferred_element_type=jnp.float32))]
  transfers between devices with their start and end apart: 3 -> 0, of which waited for: 2 -> 0; matrix products, arithmetic and copies ran while one was open for 21% -> 0% of each run, Pallas kernels for 0% -> 0%
where the time goes in v1:
time: 53.1 us; the launch traced here: 53 us
  Pallas kernels  49.3 us (93%)
  local copies, waits for them, and re-layouts  3.7 us (7%)
    pallas_call x1, Pallas kernels, per_device(): pl.pallas_call(functools.partial(kernel, n, cap, hcap), out_shape=jax.Sha...  49.3 us
    unnamed x2, local copies, waits for them, and re-layouts  3.7 us

profile of v1, /device:TPU:0, one launch (start us, length us, event | category | flops | bytes accessed | tf_op | source)
XLA Modules:
  0.0 53.0 jit_solution(12219894256424693799)
XLA Ops:
  0.0 2.0 %copy.19.refs_0_ = bf16[512,474]{1,0:T(8,128)(2,1)} copy(bf16[512,474]{0,1:T(8,128)(2,1)} %param.18) | data formatting | bytes 970752 | tf_op args[0]
  2.0 49.3 %shard_map.172 = bf16[256,512]{1,0:T(8,128)(2,1)} custom-call(bf16[512,474]{1,0:T(8,128)(2,1)} %copy.19.refs_0_, s32[1,512]{1,0:T(1,128)} %bitcast.6, s32[1,512]{1,0:T(1,128)} %bitcast.7, bf16[256,512]{1,0:T(8,128)(2,1)} %refs_3_.1, bf16[2048,512]{1,0:T(8,128)(2,1)} %refs_4_.1, s32[16,128]{1,0:T(8,128)} %bitcast.4, s32[16,128]{1,0:T(8,128)} %bitcast.5, ...), custom_call_target="tpu_custom_call" | custom-call | tf_op jit(solution)/shard_map/pallas_call | solution.py:314
  51.3 1.7 %copy.21 = bf16[256,512]{1,0:T(8,128)(2,1)} copy(bf16[256,512]{1,0:T(8,128)(2,1)} %shard_map.172) | data formatting | bytes 524288

commit v2 on v1

--- a/solution.py
+++ b/solution.py
@@ -87,6 +87,9 @@
         list_hot,
         halo_out,
         halo_in,
+        relay_out,
+        relay_in,
+        relay_sem,
         load_sem,
         row_send,
         row_recv,
@@ -95,16 +98,23 @@
         halo_send,
         halo_recv,
     ) = refs[37:]
-    grid_count = grid_in.shape[0]
+    grid_count = grid_in.shape[1]
     nodes, width = embed.shape
     edge_count = edges.shape[0]
     me = lax.axis_index("mesh")
 
-    def offset(t):
-        return n // 2 - (t + 1) // 2 if t % 2 else n // 2 + t // 2
+    half = n // 2
+    base = me // half * half
+    mirror = lax.rem(me + half, n)
+
+    def around(t, count):
+        return count // 2 - (t + 1) // 2 if t % 2 else count // 2 + t // 2
 
     def peer(t):
-        return lax.rem(me + offset(t), n)
+        return lax.rem(me + around(t, n), n)
+
+    def near_peer(t):
+        return base + lax.rem(me + around(t, half), half)
 
     loads = [
         pltpu.make_async_copy(source, target, load_sem.at[i])
@@ -118,15 +128,17 @@
 
     loads[1].wait()
     loads[2].wait()
-    step = lax.broadcasted_iota(jnp.int32, (n, 1), 0)
-    turn = n // 2 + jnp.where(step % 2 == 1, -((step + 1) // 2), step // 2)
-    target = lax.rem(me + turn, n)
+    block = lax.broadcasted_iota(jnp.int32, (n, 1), 0)
+    step = lax.rem(block, half)
+    turn = half // 2 + jnp.where(step % 2 == 1, -((step + 1) // 2), step // 2)
+    target = base + lax.rem(me + turn, half)
+    target = jnp.where(block < half, lax.rem(target + half, n), target)
     flags = jnp.where(target == owner[...], 1.0, 0.0)
     earlier = hot(
         lax.broadcasted_iota(jnp.int32, (grid_count, grid_count), 0)
         < lax.broadcasted_iota(jnp.int32, (grid_count, grid_count), 1)
     )
-    rank = dot(flags.astype(BF16), earlier) + (step * cap).astype(F32)
+    rank = dot(flags.astype(BF16), earlier) + (block * cap).astype(F32)
     place = jnp.sum(flags * rank, 0, keepdims=True).astype(jnp.int32)
     slots = (flags * (node_slot[...] + 1).astype(F32)).astype(BF16)
     lane_hot = hot(
@@ -135,31 +147,38 @@
     ids = lax.dot_general(slots, lane_hot, (((1,), (1,)), ((), ())), preferred_element_type=F32)
     for t in range(n):
         ids_out[t] = ids[t : t + 1, :]
-    ids_in[n - 1] = ids[n - 1 : n, :]
+    for t in (half - 1, n - 1):
+        ids_in[t] = ids[t : t + 1, :]
 
     loads[0].wait()
     loads[8].wait()
     loads[9].wait()
-    hidden = silu(dot(grid_in[...], w_grid_first[...])).astype(BF16)
+    hidden = lax.dot_general(
+        grid_in[...], w_grid_first[...], (((0,), (0,)), ((), ())), preferred_element_type=F32
+    )
+    hidden = silu(hidden).astype(BF16)
     latent[...] = normalize(dot(hidden, w_grid_second[...])).astype(BF16)
 
     pl.semaphore_wait(barrier, n - 1)
     per_group = GROUP // cap
-    copies = []
+    copies = {}
     for group in range(n // per_group):
         pack = hot(
             lax.broadcasted_iota(jnp.int32, (GROUP, grid_count), 0) + group * GROUP == place
         )
-        block = dot(pack, latent[...]).astype(BF16)
+        packed = dot(pack, latent[...]).astype(BF16)
         first = group * per_group
-        outgoing[first : first + per_group] = block.reshape(per_group, cap, width)
-        for t in range(first, min(first + per_group, n - 1)):
+        outgoing[first : first + per_group] = packed.reshape(per_group, cap, width)
+        for t in range(first, first + per_group):
+            if t % half == half - 1:
+                arrived[t] = outgoing[t]
+                continue
             id_copy = pltpu.make_async_remote_copy(
                 src_ref=ids_out.at[t],
                 dst_ref=ids_in.at[t],
                 send_sem=id_send.at[t],
                 recv_sem=id_recv.at[t],
-                device_id={"mesh": peer(t)},
+                device_id={"mesh": near_peer(t % half)},
                 device_id_type=MESH,
             )
             row_copy = pltpu.make_async_remote_copy(
@@ -167,19 +186,47 @@
                 dst_ref=arrived.at[t],
                 send_sem=row_send.at[t],
                 recv_sem=row_recv.at[t],
-                device_id={"mesh": peer(t)},
+                device_id={"mesh": near_peer(t % half)},
                 device_id_type=MESH,
             )
             id_copy.start()
             row_copy.start()
-            copies.append((id_copy, row_copy))
-    arrived[n - 1] = outgoing[n - 1]
+            copies[t] = (id_copy, row_copy)
 
     loads[14].wait()
     loads[4].wait()
     for chunk in range(edge_count // CHUNK):
         rows = pl.ds(chunk * CHUNK, CHUNK)
         pre[rows, :] = dot(edges[rows, :], w_edge[...])
+
+    slot_iota = lax.broadcasted_iota(jnp.int32, (nodes, GROUP), 0).astype(F32) + 1.0
+
+    def collect(start, stop):
+        total = jnp.zeros((nodes, width), F32)
+        for first in range(start, stop, per_group):
+            named = jnp.zeros((1, GROUP), F32)
+            for t in range(first, first + per_group):
+                if t in copies:
+                    copies[t][0].wait_recv()
+                    copies[t][1].wait_recv()
+                named = named + ids_in[t]
+            total = total + dot(
+                hot(slot_iota == named),
+                arrived[first : first + per_group].reshape(GROUP, width),
+            )
+        return total
+
+    relay_out[...] = collect(0, half).astype(BF16)
+    relay = pltpu.make_async_remote_copy(
+        src_ref=relay_out,
+        dst_ref=relay_in,
+        send_sem=relay_sem.at[0],
+        recv_sem=relay_sem.at[1],
+        device_id={"mesh": mirror},
+        device_id_type=MESH,
+    )
+    relay.start()
+
     loads[5].wait()
     loads[6].wait()
     loads[7].wait()
@@ -203,20 +250,9 @@
     for p in range(n):
         list_hot[p * hcap : (p + 1) * hcap, :] = hot(list_columns[:, p : p + 1] == list_iota)
 
-    gathered = jnp.zeros((nodes, width), F32)
-    slot_iota = lax.broadcasted_iota(jnp.int32, (nodes, GROUP), 0).astype(F32) + 1.0
-    for group in range(n // per_group):
-        first = group * per_group
-        named = jnp.zeros((1, GROUP), F32)
-        for t in range(first, first + per_group):
-            if t < n - 1:
-                copies[t][0].wait_recv()
-                copies[t][1].wait_recv()
-            named = named + ids_in[t]
-        gathered = gathered + dot(
-            hot(slot_iota == named),
-            arrived[first : first + per_group].reshape(GROUP, width),
-        )
+    gathered = collect(half, n)
+    relay.wait_recv()
+    gathered = gathered + relay_in[...].astype(F32)
 
     for i in (3, 10, 11, 12, 13):
         loads[i].wait()
@@ -256,7 +292,8 @@
         loads[i].wait()
     node_sum = dot(summed.astype(BF16), w_message[...])
     out_ref[...] = update(state, node_sum, w_proc_first, w_proc_second)
-    for id_copy, row_copy in copies:
+    relay.wait_send()
+    for id_copy, row_copy in copies.values():
         id_copy.wait_send()
         row_copy.wait_send()
     for copy in halo_copies:
@@ -279,7 +316,7 @@
         senders = jnp.where(senders < nodes, senders, moved)
         send_list = jnp.pad(send_list, ((0, 0), (0, hcap - list_size)))
     inputs = (
-        grid_in,
+        grid_in.T,
         owner.reshape(1, grid_count),
         node_slot.reshape(1, grid_count),
         mesh_embed,
@@ -303,6 +340,9 @@
         pltpu.VMEM((n * hcap, nodes), BF16),
         pltpu.VMEM((n, hcap, width), BF16),
         pltpu.VMEM((n, hcap, width), BF16),
+        pltpu.VMEM((nodes, width), BF16),
+        pltpu.VMEM((nodes, width), BF16),
+        dma((2,)),
         dma((len(inputs),)),
         dma((n,)),
         dma((n,)),

time: 53.1 us -> 49.9 us (0.940)
  local copies, waits for them, and re-layouts: 3.7 us -> 1.67 us
  Pallas kernels: 49.3 us -> 48.1 us
    unnamed x2 -> x1, local copies, waits for them, and re-layouts: 3.7 us -> 1.67 us
    pallas_call x1, Pallas kernels: 49.3 us -> 48.1 us  [per_device(): pl.pallas_call(functools.partial(kernel, n, cap, hcap), out_shape=jax.Sha...]
where the time goes in v2:
time: 49.9 us; the launch traced here: 49.8 us
  Pallas kernels  48.1 us (96%)
  local copies, waits for them, and re-layouts  1.67 us (3%)
    pallas_call x1, Pallas kernels, per_device(): pl.pallas_call(functools.partial(kernel, n, cap, hcap), out_shape=jax.Sha...  48.1 us
    unnamed x1, local copies, waits for them, and re-layouts  1.67 us

profile of v2, /device:TPU:0, one launch (start us, length us, event | category | flops | bytes accessed | tf_op | source)
XLA Modules:
  0.0 49.8 jit_solution(5755746473331484275)
XLA Ops:
  0.0 48.1 %shard_map.172 = bf16[256,512]{1,0:T(8,128)(2,1)} custom-call(bf16[474,512]{1,0:T(8,128)(2,1)} %bitcast.5, s32[1,512]{1,0:T(1,128)} %bitcast.8, s32[1,512]{1,0:T(1,128)} %bitcast.9, bf16[256,512]{1,0:T(8,128)(2,1)} %refs_3_.1, bf16[2048,512]{1,0:T(8,128)(2,1)} %refs_4_.1, s32[16,128]{1,0:T(8,128)} %bitcast.6, s32[16,128]{1,0:T(8,128)} %bitcast.7, ...), custom_call_target="tpu_custom_call" | custom-call | tf_op jit(solution)/shard_map/pallas_call | solution.py:354
  48.1 1.7 %copy.20 = bf16[256,512]{1,0:T(8,128)(2,1)} copy(bf16[256,512]{1,0:T(8,128)(2,1)} %shard_map.172) | data formatting | bytes 524288

commit v3 on v2

--- a/solution.py
+++ b/solution.py
@@ -107,6 +107,9 @@
     base = me // half * half
     mirror = lax.rem(me + half, n)
 
+    def direct(place):
+        return (1 - place % 2) * (1 - place % half // (half // 2))
+
     def around(t, count):
         return count // 2 - (t + 1) // 2 if t % 2 else count // 2 + t // 2
 
@@ -147,8 +150,7 @@
     ids = lax.dot_general(slots, lane_hot, (((1,), (1,)), ((), ())), preferred_element_type=F32)
     for t in range(n):
         ids_out[t] = ids[t : t + 1, :]
-    for t in (half - 1, n - 1):
-        ids_in[t] = ids[t : t + 1, :]
+    ids_in[n - 1] = ids[n - 1 : n, :]
 
     loads[0].wait()
     loads[8].wait()
@@ -170,15 +172,18 @@
         first = group * per_group
         outgoing[first : first + per_group] = packed.reshape(per_group, cap, width)
         for t in range(first, first + per_group):
-            if t % half == half - 1:
+            if t == n - 1:
                 arrived[t] = outgoing[t]
                 continue
+            receiver = near_peer(t % half)
+            if t < half:
+                receiver = lax.rem(receiver + half * direct(receiver), n)
             id_copy = pltpu.make_async_remote_copy(
                 src_ref=ids_out.at[t],
                 dst_ref=ids_in.at[t],
                 send_sem=id_send.at[t],
                 recv_sem=id_recv.at[t],
-                device_id={"mesh": near_peer(t % half)},
+                device_id={"mesh": mirror if t == half - 1 else receiver},
                 device_id_type=MESH,
             )
             row_copy = pltpu.make_async_remote_copy(
@@ -186,12 +191,24 @@
                 dst_ref=arrived.at[t],
                 send_sem=row_send.at[t],
                 recv_sem=row_recv.at[t],
-                device_id={"mesh": near_peer(t % half)},
+                device_id={"mesh": mirror if t == half - 1 else receiver},
                 device_id_type=MESH,
             )
-            id_copy.start()
-            row_copy.start()
             copies[t] = (id_copy, row_copy)
+            if t == half - 1:
+
+                @pl.when(direct(me) == 1)
+                def _():
+                    copies[half - 1][0].start()
+                    copies[half - 1][1].start()
+
+                @pl.when(direct(me) == 0)
+                def _():
+                    ids_in[half - 1] = ids_out[half - 1]
+                    arrived[half - 1] = outgoing[half - 1]
+            else:
+                id_copy.start()
+                row_copy.start()
 
     loads[14].wait()
     loads[4].wait()
@@ -206,7 +223,13 @@
         for first in range(start, stop, per_group):
             named = jnp.zeros((1, GROUP), F32)
             for t in range(first, first + per_group):
-                if t in copies:
+                if t == half - 1:
+
+                    @pl.when(direct(me) == 1)
+                    def _():
+                        copies[half - 1][0].wait_recv()
+                        copies[half - 1][1].wait_recv()
+                elif t in copies:
                     copies[t][0].wait_recv()
                     copies[t][1].wait_recv()
                 named = named + ids_in[t]
@@ -225,7 +248,14 @@
         device_id={"mesh": mirror},
         device_id_type=MESH,
     )
-    relay.start()
+
+    @pl.when(direct(me) == 0)
+    def _():
+        relay.start()
+
+    @pl.when(direct(me) == 1)
+    def _():
+        relay_in[...] = relay_out[...]
 
     loads[5].wait()
     loads[6].wait()
@@ -251,7 +281,11 @@
         list_hot[p * hcap : (p + 1) * hcap, :] = hot(list_columns[:, p : p + 1] == list_iota)
 
     gathered = collect(half, n)
-    relay.wait_recv()
+
+    @pl.when(direct(me) == 0)
+    def _():
+        relay.wait_recv()
+
     gathered = gathered + relay_in[...].astype(F32)
 
     for i in (3, 10, 11, 12, 13):
@@ -292,10 +326,20 @@
         loads[i].wait()
     node_sum = dot(summed.astype(BF16), w_message[...])
     out_ref[...] = update(state, node_sum, w_proc_first, w_proc_second)
-    relay.wait_send()
-    for id_copy, row_copy in copies.values():
-        id_copy.wait_send()
-        row_copy.wait_send()
+
+    @pl.when(direct(me) == 0)
+    def _():
+        relay.wait_send()
+
+    @pl.when(direct(me) == 1)
+    def _():
+        copies[half - 1][0].wait_send()
+        copies[half - 1][1].wait_send()
+
+    for t, (id_copy, row_copy) in copies.items():
+        if t != half - 1:
+            id_copy.wait_send()
+            row_copy.wait_send()
     for copy in halo_copies:
         copy.wait_send()
 

time: 49.9 us -> 48.4 us (0.970)
  Pallas kernels: 48.1 us -> 46.6 us
    pallas_call x1, Pallas kernels: 48.1 us -> 46.6 us  [per_device(): pl.pallas_call(functools.partial(kernel, n, cap, hcap), out_shape=jax.Sha...]
where the time goes in v3:
time: 48.4 us; the launch traced here: 48.3 us
  Pallas kernels  46.6 us (96%)
  local copies, waits for them, and re-layouts  1.67 us (3%)
    pallas_call x1, Pallas kernels, per_device(): pl.pallas_call(functools.partial(kernel, n, cap, hcap), out_shape=jax.Sha...  46.6 us
    unnamed x1, local copies, waits for them, and re-layouts  1.67 us

profile of v3, /device:TPU:0, one launch (start us, length us, event | category | flops | bytes accessed | tf_op | source)
XLA Modules:
  0.0 48.3 jit_solution(10448776326708909052)
XLA Ops:
  0.0 46.6 %shard_map.172 = bf16[256,512]{1,0:T(8,128)(2,1)} custom-call(bf16[474,512]{1,0:T(8,128)(2,1)} %bitcast.5, s32[1,512]{1,0:T(1,128)} %bitcast.8, s32[1,512]{1,0:T(1,128)} %bitcast.9, bf16[256,512]{1,0:T(8,128)(2,1)} %refs_3_.1, bf16[2048,512]{1,0:T(8,128)(2,1)} %refs_4_.1, s32[16,128]{1,0:T(8,128)} %bitcast.6, s32[16,128]{1,0:T(8,128)} %bitcast.7, ...), custom_call_target="tpu_custom_call" | custom-call | tf_op jit(solution)/shard_map/pallas_call | solution.py:398
  46.6 1.7 %copy.20 = bf16[256,512]{1,0:T(8,128)(2,1)} copy(bf16[256,512]{1,0:T(8,128)(2,1)} %shard_map.172) | data formatting | bytes 524288

commit v4 on v3

--- a/solution.py
+++ b/solution.py
@@ -264,7 +264,14 @@
     receiver_columns = jnp.transpose(receivers[...])
     list_columns = jnp.transpose(send_list[...])
     near_iota = lax.broadcasted_iota(jnp.int32, (LANES, nodes), 1)
-    halo_iota = lax.broadcasted_iota(jnp.int32, (LANES, n * hcap), 1) + nodes
+    lane = lax.broadcasted_iota(jnp.int32, (1, n * hcap), 1)
+    slot = lane // hcap
+    near = slot // half
+    back = slot % half
+    back = half // 2 + jnp.where(back % 2 == 1, -((back + 1) // 2), back // 2)
+    source = base + lax.rem(me + n - back, half)
+    source = jnp.where(near == 1, source, lax.rem(source + half, n))
+    halo_place = nodes + source * hcap + lane % hcap
     node_iota = lax.broadcasted_iota(jnp.int32, (nodes, LANES), 0)
     for part in range(edge_count // LANES):
         rows = pl.ds(part * LANES, LANES)
@@ -272,7 +279,7 @@
         receiver = receiver_columns[:, part : part + 1]
         near_hot[rows, :nodes] = hot(sender == near_iota)
         near_hot[rows, nodes:] = hot(receiver == near_iota)
-        halo_hot[rows, :] = hot(sender == halo_iota)
+        halo_hot[rows, :] = hot(sender == halo_place)
         node_hot[:, part * LANES : (part + 1) * LANES] = hot(
             receivers[part : part + 1, :] == node_iota
         )
@@ -293,32 +300,43 @@
     state = update(embed[...], gathered, w_enc_first, w_enc_second)
     sent = dot(state, w_send[...]).astype(BF16)
     halo_out[...] = dot(list_hot[...], sent).astype(BF16).reshape(n, hcap, width)
-    halo_copies = []
-    for t in range(n - 1):
-        copy = pltpu.make_async_remote_copy(
-            src_ref=halo_out.at[peer(t)],
-            dst_ref=halo_in.at[me],
-            send_sem=halo_send.at[t],
-            recv_sem=halo_recv.at[t],
-            device_id={"mesh": peer(t)},
-            device_id_type=MESH,
-        )
-        copy.start()
-        halo_copies.append(copy)
-    halo_in[me] = halo_out[me]
+    halo_copies = {}
+    for t in range(half):
+        for far in (1, 0):
+            slot = t if far else half + t
+            if slot == n - 1:
+                continue
+            receiver = lax.rem(near_peer(t) + half * far, n)
+            halo_copies[slot] = pltpu.make_async_remote_copy(
+                src_ref=halo_out.at[receiver],
+                dst_ref=halo_in.at[slot],
+                send_sem=halo_send.at[slot],
+                recv_sem=halo_recv.at[slot],
+                device_id={"mesh": receiver},
+                device_id_type=MESH,
+            )
+            halo_copies[slot].start()
+    halo_in[n - 1] = halo_out[me]
     local_table[:nodes, :] = sent
     local_table[nodes:, :] = dot(state, w_recv[...]).astype(BF16)
     for chunk in range(edge_count // CHUNK):
         rows = pl.ds(chunk * CHUNK, CHUNK)
         pre[rows, :] += dot(near_hot[rows, :], local_table[...])
 
-    for copy in halo_copies:
-        copy.wait_recv()
-    halo = halo_in[...].reshape(n * hcap, width)
+    for slot in range(half, n - 1):
+        halo_copies[slot].wait_recv()
+    inner = half * hcap
+    halo = halo_in[half:].reshape(inner, width)
+    for chunk in range(edge_count // CHUNK):
+        rows = pl.ds(chunk * CHUNK, CHUNK)
+        pre[rows, :] += dot(halo_hot[rows, inner:], halo)
+    for slot in range(half):
+        halo_copies[slot].wait_recv()
+    halo = halo_in[:half].reshape(inner, width)
     summed = jnp.zeros((nodes, width), F32)
     for chunk in range(edge_count // CHUNK):
         rows = pl.ds(chunk * CHUNK, CHUNK)
-        edge_pre = pre[rows, :] + dot(halo_hot[rows, :], halo)
+        edge_pre = pre[rows, :] + dot(halo_hot[rows, :inner], halo)
         summed = summed + dot(
             node_hot[:, chunk * CHUNK : (chunk + 1) * CHUNK], silu(edge_pre).astype(BF16)
         )
@@ -340,7 +358,7 @@
         if t != half - 1:
             id_copy.wait_send()
             row_copy.wait_send()
-    for copy in halo_copies:
+    for copy in halo_copies.values():
         copy.wait_send()
 
 

time: 48.4 us -> 45.9 us (0.948)
  Pallas kernels: 46.6 us -> 44.1 us
    pallas_call x1, Pallas kernels: 46.6 us -> 44.1 us  [per_device(): pl.pallas_call(functools.partial(kernel, n, cap, hcap), out_shape=jax.Sha...]
where the time goes in v4:
time: 45.9 us; the launch traced here: 45.7 us
  Pallas kernels  44.1 us (96%)
  local copies, waits for them, and re-layouts  1.67 us (4%)
    pallas_call x1, Pallas kernels, per_device(): pl.pallas_call(functools.partial(kernel, n, cap, hcap), out_shape=jax.Sha...  44.1 us
    unnamed x1, local copies, waits for them, and re-layouts  1.67 us

profile of v4, /device:TPU:0, one launch (start us, length us, event | category | flops | bytes accessed | tf_op | source)
XLA Modules:
  0.0 45.7 jit_solution(6603781166988213589)
XLA Ops:
  0.0 44.1 %shard_map.172 = bf16[256,512]{1,0:T(8,128)(2,1)} custom-call(bf16[474,512]{1,0:T(8,128)(2,1)} %bitcast.5, s32[1,512]{1,0:T(1,128)} %bitcast.8, s32[1,512]{1,0:T(1,128)} %bitcast.9, bf16[256,512]{1,0:T(8,128)(2,1)} %refs_3_.1, bf16[2048,512]{1,0:T(8,128)(2,1)} %refs_4_.1, s32[16,128]{1,0:T(8,128)} %bitcast.6, s32[16,128]{1,0:T(8,128)} %bitcast.7, ...), custom_call_target="tpu_custom_call" | custom-call | tf_op jit(solution)/shard_map/pallas_call | solution.py:416
  44.1 1.7 %copy.20 = bf16[256,512]{1,0:T(8,128)(2,1)} copy(bf16[256,512]{1,0:T(8,128)(2,1)} %shard_map.172) | data formatting | bytes 524288
